TPU v7x, 256 devices: a whole 4x4x8 slice. The times are simulated.
256 devices in a mesh: sec: 64 (over y, z, core), op: 4 (over x).
Axes of the slice: x: 4, y: 4, z: 8, core: 2. Of those that a mesh axis runs over, the one named last changes fastest.
Arguments:
- wave: bfloat16 [384, 256, 256], P('sec', 'op'), may hold values from -6 to 6
- left_ops: bfloat16 [384, 32, 256, 256], P('sec', 'op'), may hold values from -0.09375 to 0.09375
- right_ops: bfloat16 [384, 32, 256, 256], P('sec', 'op'), may hold values from -0.375 to 0.375
- owner_map: int32 [384, 5], P('sec'), may hold values from 0 to 63, all different within a row; in each aligned block of 6 rows (0 to 5, 6 to 11, ...) at most 2 rows name the same one
- local_map: int32 [384, 5], P('sec'), may hold values from 0 to 5
- op_class: int32 [32], P('op'), may hold values from 0 to 4
Outputs:
- applied: bfloat16 [384, 256, 256], P('sec', 'op')
Inputs may be any that keep to these rules, and one draw needn't show every extreme that they name: `owner_map`: each row names 5 different owners; among the rows of one sec index no owner is named more than 2 times, and that count is reached.
All inputs are finite; a program needn't handle non-finite values.
Results may differ from a plain program's by a relative error of at most 0.0049.
Values may be sent and summed in bfloat16 or wider, within the bound.
A program may use at most 128 MiB of HBM per device.

v0:
```python
import jax
import jax.numpy as jnp
from jax import lax
from jax.sharding import PartitionSpec as P


def shards(wave, left_ops, right_ops, owner_map, local_map, op_class):
    sec_size = lax.axis_size("sec")
    sec_dev, classes = owner_map.shape
    block_size = left_ops.shape[2]
    request_count = sec_dev * classes
    capacity = max(2, (request_count + sec_size - 1) // sec_size + 1)
    owners = owner_map.reshape(request_count)
    local_rows = local_map.reshape(request_count)
    devices = jnp.arange(sec_size, dtype=jnp.int32)
    onehot = (owners[:, None] == devices[None, :]).astype(jnp.int32)
    before = jnp.cumsum(onehot, axis=0) - onehot
    ranks_in = jnp.sum(before * onehot, axis=1)
    slot_of = owners * capacity + ranks_in
    request_table = jnp.full((sec_size * capacity,), -1, jnp.int32).at[slot_of].set(local_rows)
    wanted = lax.all_to_all(
        request_table.reshape(sec_size, capacity), "sec", split_axis=0, concat_axis=0, tiled=True
    )
    block_index = jnp.maximum(wanted, 0).reshape(sec_size * capacity)
    full_wave = lax.all_gather(wave, "op", axis=1, tiled=True)
    outgoing = full_wave[block_index].reshape(sec_size, capacity, block_size, block_size)
    fetched = lax.all_to_all(outgoing, "sec", split_axis=0, concat_axis=0, tiled=True)
    fetched = fetched.reshape(sec_size * capacity, block_size, block_size)
    sources = fetched[slot_of].reshape(sec_dev, classes, block_size, block_size)
    chosen = sources[:, op_class]
    lifted = jnp.einsum(
        "tonk,tokm->tonm", left_ops, chosen, preferred_element_type=jnp.float32
    ).astype(jnp.bfloat16)
    partial_value = jnp.einsum(
        "tonm,tokm->tnk", lifted, right_ops, preferred_element_type=jnp.float32
    )
    return lax.psum_scatter(partial_value, "op", scatter_dimension=1, tiled=True).astype(
        jnp.bfloat16
    )


def solution(mesh):
    in_specs = (
        P("sec", "op", None),
        P("sec", "op", None, None),
        P("sec", "op", None, None),
        P("sec", None),
        P("sec", None),
        P("op"),
    )
    out_specs = P("sec", "op", None)
    return jax.shard_map(shards, mesh=mesh, in_specs=in_specs, out_specs=out_specs, check_vma=False)
```

profile of v0, /device:TPU:2, one launch (start us, length us, event | category | flops | bytes accessed | tf_op | source)
XLA Modules:
  0.0 477.5 jit_solution(1271611467882633533)
XLA Ops:
  6.5 0.8 eq.15
  7.3 0.7 broadcast_multiply_fusion
  8.0 0.1 fusion.14
  8.1 0.1 reduce_window_sum.11
  8.1 0.2 select_reduce_fusion
  8.3 0.1 mul.17
  8.4 0.8 reshape.92
  9.2 0.7 scatter_custom_fusion
  9.8 0.8 all_to_all.9
  10.6 12.1 %all-to-all-start = ((s32[64,1,2]{2,1,0:T(1,128)}), s32[64,1,2]{2,1,0:T(1,128)S(1)}, u32[]{:S(2)}, u32[]{:S(2)}) async-start(s32[64,1,2]{2,1,0:T(1,128)} %bitcast.2), calls=%async_computation | async-start | bytes 65536 | tf_op jit(solution)/shard_map/all_to_all | solution.py:21
  22.7 14.4 %all_gather.3 = bf16[6,256,256]{2,1,0:T(8,128)(2,1)S(1)} all-gather(bf16[6,64,256]{2,1,0:T(8,128)(2,1)} %param.6), channel_id=1, replica_groups=mesh['sec'=64,'op'=4] {'op'}, dimensions={1}, use_global_device_ids=true | all-gather | bytes 983040 | tf_op jit(solution)/shard_map/all_gather | solution.py:25
  37.1 0.0 all-to-all-done
  37.1 0.1 maximum_reduce_fusion
  37.2 0.1 reshape.66
  37.3 7.9 %gather_fusion = bf16[128,256,256]{2,1,0:T(8,128)(2,1)} fusion(bf16[6,256,256]{2,1,0:T(8,128)(2,1)S(1)} %all_gather.3, s32[1024]{0:T(1024)S(1)} %pad_clamp_fusion.2), kind=kCustom, calls=%fused_computation | custom fusion | bytes 33554944 | tf_op jit(solution)/shard_map/gather | solution.py:26
  45.3 0.0 copy-start
  45.3 10.8 %all-to-all-start.1 = ((bf16[64,2,256,256]{3,2,1,0:T(8,128)(2,1)}), bf16[64,2,256,256]{3,2,1,0:T(8,128)(2,1)}, u32[]{:S(2)}, u32[]{:S(2)}) async-start(bf16[64,2,256,256]{3,2,1,0:T(8,128)(2,1)} %bitcast.25), calls=%async_computation.1 | async-start | bytes 33554432 | tf_op jit(solution)/shard_map/all_to_all | solution.py:27
  56.1 0.0 reduce-scatter.2.cloned.1.call-start
  56.1 0.0 copy-done
  56.2 364.5 %all-to-all-done.1 = bf16[64,2,256,256]{3,2,1,0:T(8,128)(2,1)} async-done(((bf16[64,2,256,256]{3,2,1,0:T(8,128)(2,1)}), bf16[64,2,256,256]{3,2,1,0:T(8,128)(2,1)}, u32[]{:S(2)}, u32[]{:S(2)}) %all-to-all-start.1) | async-done | bytes 16777248 | tf_op jit(solution)/shard_map/all_to_all | solution.py:27
  420.7 8.5 %gather_fusion.1 = bf16[30,256,256]{2,1,0:T(8,128)(2,1)} fusion(bf16[128,256,256]{2,1,0:T(8,128)(2,1)} %bitcast.4, s32[1024]{0:T(1024)S(1)} %pad_clamp_fusion.1), kind=kCustom, calls=%fused_computation.1 | custom fusion | bytes 7864440 | tf_op jit(solution)/shard_map/gather | solution.py:29
  429.1 5.7 %gather_fusion.2 = bf16[8,6,256,256]{3,2,1,0:T(8,128)(2,1)} fusion(bf16[6,5,256,256]{3,2,1,0:T(8,128)(2,1)} %bitcast.26, s32[1024]{0:T(1024)S(1)} %pad_clamp_fusion), kind=kCustom, calls=%fused_computation.2 | custom fusion | bytes 12582944 | tf_op jit(solution)/shard_map/gather | solution.py:30
  434.9 9.6 %fusion.9 = f32[6,256,256]{2,1,0:T(8,128)} fusion(bf16[6,8,256,256]{3,2,1,0:T(8,128)(2,1)} %param.8, bf16[6,8,256,256]{3,2,1,0:T(8,128)(2,1)} %param.7, bf16[8,6,256,256]{3,2,1,0:T(8,128)(2,1)} %gather_fusion.2), kind=kOutput, calls=%fused_computation.9 | convolution fusion | flops 3224371200 | bytes 20447232 | tf_op jit(solution)/shard_map/tonm,tokm->tnk/dot_general | solution.py:34
  444.4 0.0 reduce-scatter.2.cloned.1.call-update
  444.4 24.5 %reduce-scatter.2.cloned.1.call-done = f32[6,64,256]{2,1,0:T(8,128)} async-done(((f32[6,256,256]{2,1,0:T(8,128)}), f32[6,64,256]{2,1,0:T(8,128)}) %reduce-scatter.2.cloned.1.call-update) | async-done | bytes 393232 | tf_op jit(solution)/shard_map/reduce_scatter | solution.py:37
  468.9 1.7 convert_element_type.15
  (5 shorter events, 0.0 us)
Async XLA Ops:
  10.6 26.5 %all-to-all-start = ((s32[64,1,2]{2,1,0:T(1,128)}), s32[64,1,2]{2,1,0:T(1,128)S(1)}, u32[]{:S(2)}, u32[]{:S(2)}) async-start(s32[64,1,2]{2,1,0:T(1,128)} %bitcast.2), calls=%async_computation | async-start | bytes 65536 | tf_op jit(solution)/shard_map/all_to_all | solution.py:21
  45.3 10.9 %copy-start = (s32[8]{0:T(128)S(1)}, s32[8]{0:T(128)}, u32[]{:S(2)}) copy-start(s32[8]{0:T(128)} %param.11) | copy-start | bytes 100
  45.3 375.4 %all-to-all-start.1 = ((bf16[64,2,256,256]{3,2,1,0:T(8,128)(2,1)}), bf16[64,2,256,256]{3,2,1,0:T(8,128)(2,1)}, u32[]{:S(2)}, u32[]{:S(2)}) async-start(bf16[64,2,256,256]{3,2,1,0:T(8,128)(2,1)} %bitcast.25), calls=%async_computation.1 | async-start | bytes 33554432 | tf_op jit(solution)/shard_map/all_to_all | solution.py:27
  56.1 412.9 %reduce-scatter.2.cloned.1.call-start = ((), (), s32[]{:S(2)}) async-start(), calls=%async_computation.3 | async-start | bytes 1966080 | tf_op jit(solution)/shard_map/reduce_scatter | solution.py:37
Sparse Core Ops, SparseCore 0:
  444.6 24.3 reduce-scatter.1
where the time goes:
time: 479 us; the launch traced here: 477 us
  waiting for transfers between devices  389 us (81%)
  local copies, waits for them, and re-layouts  25.3 us (5%)
  starting transfers between devices  22.9 us (5%)
  blocking collectives  14.4 us (3%)
  between operations  13.5 us (3%)
  matrix products  9.56 us (2%)
    all_to_all x1, waiting for transfers between devices, shards(): lax.all_to_all(outgoing, 'sec', split_axis=0, concat_axis=0, tiled=True)  364 us
    reduce_scatter x1, waiting for transfers between devices, shards(): lax.psum_scatter(partial_value, 'op', scatter_dimension=1, tiled=True)  24.5 us
    all_gather x1, blocking collectives, shards(): full_wave = lax.all_gather(wave, 'op', axis=1, tiled=True)  14.4 us
    all_to_all x1, starting transfers between devices, shards(): lax.all_to_all(request_table.reshape(sec_size, capacity), 'sec', split_ax...  12.1 us
    all_to_all x1, starting transfers between devices, shards(): lax.all_to_all(outgoing, 'sec', split_axis=0, concat_axis=0, tiled=True)  10.8 us
  transfers between devices with their start and end apart: 3, of which 2 were waited for; matrix products, arithmetic and copies ran while one was open for 0% of the time, Pallas kernels for 0%

commit v1 on v0

--- a/solution.py
+++ b/solution.py
@@ -22,11 +22,13 @@
         request_table.reshape(sec_size, capacity), "sec", split_axis=0, concat_axis=0, tiled=True
     )
     block_index = jnp.maximum(wanted, 0).reshape(sec_size * capacity)
-    full_wave = lax.all_gather(wave, "op", axis=1, tiled=True)
-    outgoing = full_wave[block_index].reshape(sec_size, capacity, block_size, block_size)
+    rows = wave.shape[1]
+    outgoing = wave[block_index].reshape(sec_size, capacity, rows, block_size)
     fetched = lax.all_to_all(outgoing, "sec", split_axis=0, concat_axis=0, tiled=True)
-    fetched = fetched.reshape(sec_size * capacity, block_size, block_size)
-    sources = fetched[slot_of].reshape(sec_dev, classes, block_size, block_size)
+    fetched = fetched.reshape(sec_size * capacity, rows, block_size)
+    compact = fetched[slot_of]
+    sources = lax.all_gather(compact, "op", axis=1, tiled=True)
+    sources = sources.reshape(sec_dev, classes, block_size, block_size)
     chosen = sources[:, op_class]
     lifted = jnp.einsum(
         "tonk,tokm->tonm", left_ops, chosen, preferred_element_type=jnp.float32

time: 479 us -> 238 us (0.50)
  waiting for transfers between devices: 389 us -> 168 us
  starting transfers between devices: 22.9 us -> 5.87 us
  local copies, waits for them, and re-layouts: 25.3 us -> 14.8 us
  blocking collectives: 14.4 us -> 21.4 us
    all_to_all x1, waiting for transfers between devices: 364 us -> 95.6 us  [shards(): lax.all_to_all(outgoing, 'sec', split_axis=0, concat_axis=0, tiled=True)]
    all_gather x0 -> x1, waiting for transfers between devices: none -> 44.8 us  [shards(): sources = lax.all_gather(compact, 'op', axis=1, tiled=True)]
    all_to_all x0 -> x1, blocking collectives: none -> 21.4 us  [shards(): lax.all_to_all(request_table.reshape(sec_size, capacity), 'sec', split_ax...]
    all_gather x1 -> x0, blocking collectives: 14.4 us -> none  [shards(): full_wave = lax.all_gather(wave, 'op', axis=1, tiled=True)]
    all_to_all x1 -> x0, starting transfers between devices: 12.1 us -> none  [shards(): lax.all_to_all(request_table.reshape(sec_size, capacity), 'sec', split_ax...]
    gather x2, local copies, waits for them, and re-layouts: 16.4 us -> 6.53 us  [the longest x1 3.75 us: shards(): compact = fetched[slot_of]]
    all_to_all x1, starting transfers between devices: 10.8 us -> 5.79 us  [shards(): lax.all_to_all(outgoing, 'sec', split_axis=0, concat_axis=0, tiled=True)]
  transfers between devices with their start and end apart: 3 -> 3, of which waited for: 2 -> 3; matrix products, arithmetic and copies ran while one was open for 0% -> 0% of each run, Pallas kernels for 0% -> 0%
where the time goes in v1:
time: 238 us; the launch traced here: 236 us
  waiting for transfers between devices  168 us (71%)
  blocking collectives  21.4 us (9%)
  local copies, waits for them, and re-layouts  14.8 us (6%)
  between operations  13.5 us (6%)
  matrix products  9.56 us (4%)
  starting transfers between devices  5.87 us (2%)
  other arithmetic  2.82 us (1%)
    all_to_all x1, waiting for transfers between devices, shards(): lax.all_to_all(outgoing, 'sec', split_axis=0, concat_axis=0, tiled=True)  95.6 us
    all_gather x1, waiting for transfers between devices, shards(): sources = lax.all_gather(compact, 'op', axis=1, tiled=True)  44.8 us
    reduce_scatter x1, waiting for transfers between devices, shards(): lax.psum_scatter(partial_value, 'op', scatter_dimension=1, tiled=True)  28 us
    all_to_all x1, blocking collectives, shards(): lax.all_to_all(request_table.reshape(sec_size, capacity), 'sec', split_ax...  21.4 us
    dot_general x1, matrix products, shards(): jnp.einsum('tonm,tokm->tnk', lifted, right_ops, preferred_element_type=jn...  9.56 us
    all_to_all x1, starting transfers between devices, shards(): lax.all_to_all(outgoing, 'sec', split_axis=0, concat_axis=0, tiled=True)  5.79 us
    gather x1, local copies, waits for them, and re-layouts, shards(): chosen = sources[:, op_class]  5.72 us
  transfers between devices with their start and end apart: 3, of which 3 were waited for; matrix products, arithmetic and copies ran while one was open for 0% of the time, Pallas kernels for 0%

profile of v1, /device:TPU:2, one launch (start us, length us, event | category | flops | bytes accessed | tf_op | source)
XLA Modules:
  0.0 236.4 jit_solution(16081726220174959692)
XLA Ops:
  6.5 0.0 copy-start
  6.5 0.8 eq.15
  7.3 0.7 broadcast_multiply_fusion
  8.0 0.8 reshape.92
  8.8 0.1 mul.17
  8.9 0.1 fusion.14
  8.9 0.1 reduce_window_sum.11
  9.0 0.2 select_reduce_fusion
  9.2 0.7 scatter_custom_fusion
  9.9 0.1 all_to_all.9
  10.0 21.4 %all_to_all.14 = s32[64,1,2]{2,1,0:T(1,128)S(1)} all-to-all(s32[64,1,2]{2,1,0:T(1,128)S(1)} %bitcast.28), channel_id=1, replica_groups=mesh['sec'=64,'op'=4] {'sec'}, dimensions={0} | all-to-all | bytes 1024 | tf_op jit(solution)/shard_map/all_to_all | solution.py:21
  31.4 0.1 maximum_reduce_fusion
  31.5 0.1 reshape.66
  31.7 0.0 copy-done
  31.7 2.8 %gather_fusion = bf16[128,64,256]{2,1,0:T(8,128)(2,1)} fusion(bf16[6,64,256]{2,1,0:T(8,128)(2,1)S(1)} %copy-done, s32[1024]{0:T(1024)S(1)} %pad_clamp_fusion.2), kind=kCustom, calls=%fused_computation | custom fusion | bytes 8389120 | tf_op jit(solution)/shard_map/gather | solution.py:26
  34.5 0.0 copy-start.1
  34.5 5.8 %all-to-all-start.1 = ((bf16[64,2,64,256]{3,2,1,0:T(8,128)(2,1)}), bf16[64,2,64,256]{3,2,1,0:T(8,128)(2,1)}, u32[]{:S(2)}, u32[]{:S(2)}) async-start(bf16[64,2,64,256]{3,2,1,0:T(8,128)(2,1)} %bitcast.26), calls=%async_computation.1 | async-start | bytes 8388608 | tf_op jit(solution)/shard_map/all_to_all | solution.py:27
  40.3 0.0 all-gather.3.cloned.1.call-start
  40.3 95.6 %all-to-all-done.1 = bf16[64,2,64,256]{3,2,1,0:T(8,128)(2,1)} async-done(((bf16[64,2,64,256]{3,2,1,0:T(8,128)(2,1)}), bf16[64,2,64,256]{3,2,1,0:T(8,128)(2,1)}, u32[]{:S(2)}, u32[]{:S(2)}) %all-to-all-start.1) | async-done | bytes 4194336 | tf_op jit(solution)/shard_map/all_to_all | solution.py:27
  136.0 3.7 %gather_fusion.1 = bf16[30,64,256]{2,1,0:T(8,128)(2,1)} fusion(bf16[128,64,256]{2,1,0:T(8,128)(2,1)} %bitcast.4, s32[1024]{0:T(1024)S(1)} %pad_clamp_fusion.1), kind=kCustom, calls=%fused_computation.1 | custom fusion | bytes 1966200 | tf_op jit(solution)/shard_map/gather | solution.py:29
  139.7 0.0 all-gather.3.cloned.1.call-update
  139.7 0.0 reduce-scatter.2.cloned.1.call-start
  139.8 0.0 copy-done.1
  139.8 44.8 %all-gather.3.cloned.1.call-done = bf16[30,256,256]{2,1,0:T(8,128)(2,1)} async-done(((bf16[30,64,256]{2,1,0:T(8,128)(2,1)}), bf16[30,256,256]{2,1,0:T(8,128)(2,1)}) %all-gather.3.cloned.1.call-update) | async-done | bytes 3932176 | tf_op jit(solution)/shard_map/all_gather | solution.py:30
  184.6 5.7 %gather_fusion.2 = bf16[8,6,256,256]{3,2,1,0:T(8,128)(2,1)} fusion(bf16[6,5,256,256]{3,2,1,0:T(8,128)(2,1)} %bitcast.27, s32[1024]{0:T(1024)S(1)} %pad_clamp_fusion), kind=kCustom, calls=%fused_computation.2 | custom fusion | bytes 12582944 | tf_op jit(solution)/shard_map/gather | solution.py:32
  190.3 9.6 %fusion.9 = f32[6,256,256]{2,1,0:T(8,128)} fusion(bf16[6,8,256,256]{3,2,1,0:T(8,128)(2,1)} %param.8, bf16[6,8,256,256]{3,2,1,0:T(8,128)(2,1)} %param.7, bf16[8,6,256,256]{3,2,1,0:T(8,128)(2,1)} %gather_fusion.2), kind=kOutput, calls=%fused_computation.9 | convolution fusion | flops 3224371200 | bytes 20447232 | tf_op jit(solution)/shard_map/tonm,tokm->tnk/dot_general | solution.py:36
  199.9 0.0 reduce-scatter.2.cloned.1.call-update
  199.9 28.0 %reduce-scatter.2.cloned.1.call-done = f32[6,64,256]{2,1,0:T(8,128)} async-done(((f32[6,256,256]{2,1,0:T(8,128)}), f32[6,64,256]{2,1,0:T(8,128)}) %reduce-scatter.2.cloned.1.call-update) | async-done | bytes 393232 | tf_op jit(solution)/shard_map/reduce_scatter | solution.py:39
  227.9 1.7 convert_element_type.15
  (5 shorter events, 0.0 us)
Async XLA Ops:
  6.5 25.1 %copy-start = (bf16[6,64,256]{2,1,0:T(8,128)(2,1)S(1)}, bf16[6,64,256]{2,1,0:T(8,128)(2,1)}, u32[]{:S(2)}) copy-start(bf16[6,64,256]{2,1,0:T(8,128)(2,1)} %param.6) | copy-start | bytes 589828
  34.5 105.3 %copy-start.1 = (s32[8]{0:T(128)S(1)}, s32[8]{0:T(128)}, u32[]{:S(2)}) copy-start(s32[8]{0:T(128)} %param.11) | copy-start | bytes 100
  34.5 101.5 %all-to-all-start.1 = ((bf16[64,2,64,256]{3,2,1,0:T(8,128)(2,1)}), bf16[64,2,64,256]{3,2,1,0:T(8,128)(2,1)}, u32[]{:S(2)}, u32[]{:S(2)}) async-start(bf16[64,2,64,256]{3,2,1,0:T(8,128)(2,1)} %bitcast.26), calls=%async_computation.1 | async-start | bytes 8388608 | tf_op jit(solution)/shard_map/all_to_all | solution.py:27
  40.3 144.3 %all-gather.3.cloned.1.call-start = ((), (), s32[]{:S(2)}) async-start(), calls=%async_computation.4 | async-start | bytes 4915200 | tf_op jit(solution)/shard_map/all_gather | solution.py:30
  139.7 88.2 %reduce-scatter.2.cloned.1.call-start = ((), (), s32[]{:S(2)}) async-start(), calls=%async_computation.3 | async-start | bytes 1966080 | tf_op jit(solution)/shard_map/reduce_scatter | solution.py:39
Sparse Core Ops, SparseCore 0:
  139.8 44.6 all-gather.2
  200.0 27.8 reduce-scatter.1

commit v2 on v1

v2 whole, which is shorter than its diff:
```python
import jax
import jax.numpy as jnp
from jax import lax
from jax.sharding import PartitionSpec as P


def shards(wave, left_ops, right_ops, owner_map, local_map, op_class):
    sec_dev, classes = owner_map.shape
    block_size = left_ops.shape[2]
    source = owner_map * sec_dev + local_map
    every_wave = lax.all_gather(wave, "sec", axis=0, tiled=True)
    compact = every_wave[source.reshape(sec_dev * classes)]
    sources = lax.all_gather(compact, "op", axis=1, tiled=True)
    sources = sources.reshape(sec_dev, classes, block_size, block_size)
    chosen = sources[:, op_class]
    lifted = jnp.einsum(
        "tonk,tokm->tonm", left_ops, chosen, preferred_element_type=jnp.float32
    ).astype(jnp.bfloat16)
    partial_value = jnp.einsum(
        "tonm,tokm->tnk", lifted, right_ops, preferred_element_type=jnp.float32
    )
    return lax.psum_scatter(partial_value, "op", scatter_dimension=1, tiled=True).astype(
        jnp.bfloat16
    )


def solution(mesh):
    in_specs = (
        P("sec", "op", None),
        P("sec", "op", None, None),
        P("sec", "op", None, None),
        P("sec", None),
        P("sec", None),
        P("op"),
    )
    out_specs = P("sec", "op", None)
    return jax.shard_map(shards, mesh=mesh, in_specs=in_specs, out_specs=out_specs, check_vma=False)
```

time: 238 us -> 209 us (0.88)
  blocking collectives: 21.4 us -> 0 us
  starting transfers between devices: 5.87 us -> 0.08 us
  local copies, waits for them, and re-layouts: 14.8 us -> 12 us
    all_to_all x1 -> x0, waiting for transfers between devices: 95.6 us -> none  [shards(): lax.all_to_all(outgoing, 'sec', split_axis=0, concat_axis=0, tiled=True)]
    all_gather x0 -> x1, waiting for transfers between devices: none -> 95 us  [shards(): every_wave = lax.all_gather(wave, 'sec', axis=0, tiled=True)]
    all_to_all x1 -> x0, blocking collectives: 21.4 us -> none  [shards(): lax.all_to_all(request_table.reshape(sec_size, capacity), 'sec', split_ax...]
    all_to_all x1 -> x0, starting transfers between devices: 5.79 us -> none  [shards(): lax.all_to_all(outgoing, 'sec', split_axis=0, concat_axis=0, tiled=True)]
    gather x2 -> x1, local copies, waits for them, and re-layouts: 6.53 us -> 6.22 us  [shards(): compact = every_wave[source.reshape(sec_dev * classes)]]
  transfers between devices with their start and end apart: 3 -> 3, of which waited for: 3 -> 3; matrix products, arithmetic and copies ran while one was open for 0% -> 1% of each run, Pallas kernels for 0% -> 0%
where the time goes in v2:
time: 209 us; the launch traced here: 207 us
  waiting for transfers between devices  168 us (80%)
  between operations  13.1 us (6%)
  local copies, waits for them, and re-layouts  12 us (6%)
  matrix products  11 us (5%)
  other arithmetic  3.08 us (1%)
    all_gather x1, waiting for transfers between devices, shards(): every_wave = lax.all_gather(wave, 'sec', axis=0, tiled=True)  95 us
    all_gather x1, waiting for transfers between devices, shards(): sources = lax.all_gather(compact, 'op', axis=1, tiled=True)  44.3 us
    reduce_scatter x1, waiting for transfers between devices, shards(): lax.psum_scatter(partial_value, 'op', scatter_dimension=1, tiled=True)  28 us
    dot_general x1, matrix products, shards(): jnp.einsum('tonm,tokm->tnk', lifted, right_ops, preferred_element_type=jn...  11 us
    gather x1, local copies, waits for them, and re-layouts, shards(): compact = every_wave[source.reshape(sec_dev * classes)]  6.22 us
    gather x1, local copies, waits for them, and re-layouts, shards(): chosen = sources[:, op_class]  5.72 us
  transfers between devices with their start and end apart: 3, of which 3 were waited for; matrix products, arithmetic and copies ran while one was open for 1% of the time, Pallas kernels for 0%

profile of v2, /device:TPU:2, one launch (start us, length us, event | category | flops | bytes accessed | tf_op | source)
XLA Modules:
  0.0 207.3 jit_solution(15697537779455883157)
XLA Ops:
  6.5 0.0 all-gather.4.cloned.1.call-start
  6.5 0.7 all-gather.4.cloned.1.call-update
  7.3 0.0 all-gather.6.cloned.1.call-start
  7.3 0.7 multiply_add_fusion
  8.0 0.1 reshape.34
  8.1 95.0 %all-gather.4.cloned.1.call-done = bf16[384,64,256]{2,1,0:T(8,128)(2,1)} async-done(((bf16[6,64,256]{2,1,0:T(8,128)(2,1)}), bf16[384,64,256]{2,1,0:T(8,128)(2,1)}) %all-gather.4.cloned.1.call-update) | async-done | bytes 12582928 | tf_op jit(solution)/shard_map/all_gather | solution.py:11
  103.1 6.2 %gather_fusion = bf16[30,64,256]{2,1,0:T(8,128)(2,1)} fusion(bf16[384,64,256]{2,1,0:T(8,128)(2,1)} %all-gather.4.cloned.1.call-done, s32[1024]{0:T(1024)S(1)} %pad_clamp_fusion.1), kind=kCustom, calls=%fused_computation | custom fusion | bytes 1966200 | tf_op jit(solution)/shard_map/gather | solution.py:12
  109.3 0.0 all-gather.6.cloned.1.call-update
  109.3 0.0 reduce-scatter.2.cloned.1.call-start
  109.4 0.7 compare_select_fusion
  110.1 44.3 %all-gather.6.cloned.1.call-done = bf16[30,256,256]{2,1,0:T(8,128)(2,1)} async-done(((bf16[30,64,256]{2,1,0:T(8,128)(2,1)}), bf16[30,256,256]{2,1,0:T(8,128)(2,1)}) %all-gather.6.cloned.1.call-update) | async-done | bytes 3932176 | tf_op jit(solution)/shard_map/all_gather | solution.py:13
  154.3 5.7 %gather_fusion.1 = bf16[8,6,256,256]{3,2,1,0:T(8,128)(2,1)} fusion(bf16[6,5,256,256]{3,2,1,0:T(8,128)(2,1)} %bitcast.18, s32[1024]{0:T(1024)S(1)} %pad_clamp_fusion), kind=kCustom, calls=%fused_computation.1 | custom fusion | bytes 12582944 | tf_op jit(solution)/shard_map/gather | solution.py:15
  160.1 11.0 %fusion.9 = f32[6,256,256]{2,1,0:T(8,128)} fusion(bf16[6,8,256,256]{3,2,1,0:T(8,128)(2,1)} %param.8, bf16[6,8,256,256]{3,2,1,0:T(8,128)(2,1)} %param.7, bf16[8,6,256,256]{3,2,1,0:T(8,128)(2,1)} %gather_fusion.1), kind=kOutput, calls=%fused_computation.7 | convolution fusion | flops 3224371200 | bytes 20447232 | tf_op jit(solution)/shard_map/tonm,tokm->tnk/dot_general | solution.py:19
  171.1 0.0 reduce-scatter.2.cloned.1.call-update
  171.1 28.0 %reduce-scatter.2.cloned.1.call-done = f32[6,64,256]{2,1,0:T(8,128)} async-done(((f32[6,256,256]{2,1,0:T(8,128)}), f32[6,64,256]{2,1,0:T(8,128)}) %reduce-scatter.2.cloned.1.call-update) | async-done | bytes 393232 | tf_op jit(solution)/shard_map/reduce_scatter | solution.py:22
  199.1 1.7 convert_element_type.11
  (3 shorter events, 0.0 us)
Async XLA Ops:
  6.5 96.6 %all-gather.4.cloned.1.call-start = ((), (), s32[]{:S(2)}) async-start(), calls=%async_computation.1 | async-start | bytes 12779520 | tf_op jit(solution)/shard_map/all_gather | solution.py:11
  7.3 147.1 %all-gather.6.cloned.1.call-start = ((), (), s32[]{:S(2)}) async-start(), calls=%async_computation.3 | async-start | bytes 4915200 | tf_op jit(solution)/shard_map/all_gather | solution.py:13
  109.3 89.7 %reduce-scatter.2.cloned.1.call-start = ((), (), s32[]{:S(2)}) async-start(), calls=%async_computation.2 | async-start | bytes 1966080 | tf_op jit(solution)/shard_map/reduce_scatter | solution.py:22
Sparse Core Ops, SparseCore 0:
  10.1 92.9 all-gather.3
  109.5 44.8 all-gather.5
  171.2 27.8 reduce-scatter.1

commit v3 on v2

--- a/solution.py
+++ b/solution.py
@@ -18,10 +18,8 @@
     ).astype(jnp.bfloat16)
     partial_value = jnp.einsum(
         "tonm,tokm->tnk", lifted, right_ops, preferred_element_type=jnp.float32
-    )
-    return lax.psum_scatter(partial_value, "op", scatter_dimension=1, tiled=True).astype(
-        jnp.bfloat16
-    )
+    ).astype(jnp.bfloat16)
+    return lax.psum_scatter(partial_value, "op", scatter_dimension=1, tiled=True)
 
 
 def solution(mesh):

time: 209 us -> 204 us (0.976)
  waiting for transfers between devices: 168 us -> 164 us
    reduce_scatter x1, waiting for transfers between devices: 28 us -> 23.9 us  [shards(): lax.psum_scatter(partial_value, 'op', scatter_dimension=1, tiled=True)]
where the time goes in v3:
time: 204 us; the launch traced here: 201 us
  waiting for transfers between devices  164 us (80%)
  between operations  13.1 us (6%)
  local copies, waits for them, and re-layouts  12 us (6%)
  matrix products  10.7 us (5%)
    all_gather x1, waiting for transfers between devices, shards(): every_wave = lax.all_gather(wave, 'sec', axis=0, tiled=True)  95 us
    all_gather x1, waiting for transfers between devices, shards(): sources = lax.all_gather(compact, 'op', axis=1, tiled=True)  44.3 us
    reduce_scatter x1, waiting for transfers between devices, shards(): lax.psum_scatter(partial_value, 'op', scatter_dimension=1, tiled=True)  23.9 us
    dot_general x1, matrix products, shards(): jnp.einsum('tonm,tokm->tnk', lifted, right_ops, preferred_element_type=jn...  10.7 us
    gather x1, local copies, waits for them, and re-layouts, shards(): compact = every_wave[source.reshape(sec_dev * classes)]  6.22 us
    gather x1, local copies, waits for them, and re-layouts, shards(): chosen = sources[:, op_class]  5.72 us
  transfers between devices with their start and end apart: 3, of which 3 were waited for; matrix products, arithmetic and copies ran while one was open for 1% of the time, Pallas kernels for 0%

profile of v3, /device:TPU:2, one launch (start us, length us, event | category | flops | bytes accessed | tf_op | source)
XLA Modules:
  0.0 201.3 jit_solution(12440562342349995092)
XLA Ops:
  6.5 0.0 all-gather.4.cloned.1.call-start
  6.5 0.7 all-gather.4.cloned.1.call-update
  7.3 0.0 all-gather.6.cloned.1.call-start
  7.3 0.7 multiply_add_fusion
  8.0 0.1 reshape.34
  8.1 95.0 %all-gather.4.cloned.1.call-done = bf16[384,64,256]{2,1,0:T(8,128)(2,1)} async-done(((bf16[6,64,256]{2,1,0:T(8,128)(2,1)}), bf16[384,64,256]{2,1,0:T(8,128)(2,1)}) %all-gather.4.cloned.1.call-update) | async-done | bytes 12582928 | tf_op jit(solution)/shard_map/all_gather | solution.py:11
  103.1 6.2 %gather_fusion = bf16[30,64,256]{2,1,0:T(8,128)(2,1)} fusion(bf16[384,64,256]{2,1,0:T(8,128)(2,1)} %all-gather.4.cloned.1.call-done, s32[1024]{0:T(1024)S(1)} %pad_clamp_fusion.1), kind=kCustom, calls=%fused_computation | custom fusion | bytes 1966200 | tf_op jit(solution)/shard_map/gather | solution.py:12
  109.3 0.0 all-gather.6.cloned.1.call-update
  109.3 0.0 reduce-scatter.2.cloned.1.call-start
  109.4 0.7 compare_select_fusion
  110.1 44.3 %all-gather.6.cloned.1.call-done = bf16[30,256,256]{2,1,0:T(8,128)(2,1)} async-done(((bf16[30,64,256]{2,1,0:T(8,128)(2,1)}), bf16[30,256,256]{2,1,0:T(8,128)(2,1)}) %all-gather.6.cloned.1.call-update) | async-done | bytes 3932176 | tf_op jit(solution)/shard_map/all_gather | solution.py:13
  154.3 5.7 %gather_fusion.1 = bf16[8,6,256,256]{3,2,1,0:T(8,128)(2,1)} fusion(bf16[6,5,256,256]{3,2,1,0:T(8,128)(2,1)} %bitcast.18, s32[1024]{0:T(1024)S(1)} %pad_clamp_fusion), kind=kCustom, calls=%fused_computation.1 | custom fusion | bytes 12582944 | tf_op jit(solution)/shard_map/gather | solution.py:15
  160.1 10.7 %bitcast_convert_fusion = bf16[6,256,256]{2,1,0:T(8,128)(2,1)} fusion(bf16[6,8,256,256]{3,2,1,0:T(8,128)(2,1)} %param.8, bf16[6,8,256,256]{3,2,1,0:T(8,128)(2,1)} %param.7, bf16[8,6,256,256]{3,2,1,0:T(8,128)(2,1)} %gather_fusion.1), kind=kOutput, calls=%fused_computation.7 | convolution fusion | flops 3224764416 | bytes 19660800 | tf_op jit(solution)/shard_map/tonm,tokm->tnk/dot_general | solution.py:19
  170.8 0.0 reduce-scatter.2.cloned.1.call-update
  170.8 23.9 %reduce-scatter.2.cloned.1.call-done = bf16[6,64,256]{2,1,0:T(8,128)(2,1)} async-done(((bf16[6,256,256]{2,1,0:T(8,128)(2,1)}), bf16[6,64,256]{2,1,0:T(8,128)(2,1)}) %reduce-scatter.2.cloned.1.call-update) | async-done | bytes 196624 | tf_op jit(solution)/shard_map/reduce_scatter | solution.py:22
  (3 shorter events, 0.0 us)
Async XLA Ops:
  6.5 96.6 %all-gather.4.cloned.1.call-start = ((), (), s32[]{:S(2)}) async-start(), calls=%async_computation.1 | async-start | bytes 12779520 | tf_op jit(solution)/shard_map/all_gather | solution.py:11
  7.3 147.1 %all-gather.6.cloned.1.call-start = ((), (), s32[]{:S(2)}) async-start(), calls=%async_computation.3 | async-start | bytes 4915200 | tf_op jit(solution)/shard_map/all_gather | solution.py:13
  109.3 85.4 %reduce-scatter.2.cloned.1.call-start = ((), (), s32[]{:S(2)}) async-start(), calls=%async_computation.2 | async-start | bytes 983040 | tf_op jit(solution)/shard_map/reduce_scatter | solution.py:22
Sparse Core Ops, SparseCore 0:
  10.1 92.9 all-gather.3
  109.5 44.8 all-gather.5
  171.0 23.7 reduce-scatter.1
